TPU v7x, 32 devices: a whole 2x2x4 slice. The times are simulated.
32 devices in a mesh: pat: 4 (over z), vox: 8 (over y, x, core).
Axes of the slice: x: 2, y: 2, z: 4, core: 2. Of those that a mesh axis runs over, the one named last changes fastest.
Arguments:
- conductivity: float32 [16, 128, 128], P('vox'), may hold values from 0.3 to 1.5
- warm_forward: float32 [16, 32, 128, 128], P('vox', 'pat'), may hold values from -3 to 3
- warm_adjoint: float32 [16, 32, 128, 128], P('vox', 'pat'), may hold values from -3 to 3
- electrodes: int32 [128], replicated, may hold values from 0 to 262143
- patterns: int32 [32, 4], P('pat'), may hold values from 0 to 127, all different within a row
- observed: float32 [32], P('pat'), may hold values from -16 to 16
Outputs:
- gradient: float32 [16, 128, 128], P('vox')
- predicted: float32 [32], P('pat')
All inputs are finite; a program needn't handle non-finite values.
Results may differ from a plain program's by a relative error of at most 0.0003.
Values sent between devices are 32-bit elements; how exact they have to be, the bound alone decides.
No kernel may reach another device: no remote copies, remote signals or barrier semaphores. Data moves between devices by JAX's collectives and lax.ppermute only.
A program may use at most 64 MiB of HBM per device.

v0:
```python
import math
import jax
import jax.numpy as jnp
from jax import lax
from jax.sharding import PartitionSpec as P

ITERS = 2
leakage = 0.05


def extended(block, sides, width):
    for axis, dim in sides:
        count = lax.axis_size(axis)
        forward = [(i, i + 1) for i in range(count - 1)]
        backward = [(target, source) for source, target in forward]
        low = lax.ppermute(
            lax.slice_in_dim(block, block.shape[dim] - width, None, axis=dim), axis, forward
        )
        high = lax.ppermute(lax.slice_in_dim(block, 0, width, axis=dim), axis, backward)
        block = jnp.concatenate([low, block, high], axis=dim)
    return block


def both_sides(values, along_axis):
    lower_pad = [(0, 0)] * values.ndim
    upper_pad = [(0, 0)] * values.ndim
    lower_pad[along_axis] = (1, 0)
    upper_pad[along_axis] = (0, 1)
    return jnp.pad(values, lower_pad) + jnp.pad(values, upper_pad)


def spread(values, along_axis):
    lower_pad = [(0, 0)] * values.ndim
    upper_pad = [(0, 0)] * values.ndim
    lower_pad[along_axis] = (1, 0)
    upper_pad[along_axis] = (0, 1)
    return jnp.pad(values, lower_pad) - jnp.pad(values, upper_pad)


def operate(values, coeffs):
    depth_faces, row_faces, column_faces = coeffs
    padded = extended(values, (("vox", 0),), 1)
    flux_depth = depth_faces[:, None] * (padded[1:] - padded[:-1])
    result = leakage * values + (flux_depth[:-1] - flux_depth[1:])
    result = result + spread(row_faces[:, None] * (values[:, :, 1:] - values[:, :, :-1]), 2)
    result = result + spread(
        column_faces[:, None] * (values[:, :, :, 1:] - values[:, :, :, :-1]), 3
    )
    return result


def inner(left_factor, right_factor):
    return jnp.sum(left_factor * right_factor, axis=(0, 2, 3))


def widen(vector):
    return vector[None, :, None, None]


def pattern_sum(local_terms):
    return lax.psum(local_terms, "vox")


def solve_pattern(right_side, initial, coeffs, diagonal):
    solution = initial
    residue = right_side - operate(solution, coeffs)
    precond = residue / diagonal
    direction = precond
    current = pattern_sum(inner(residue, precond))
    for iteration in range(ITERS):
        applied = operate(direction, coeffs)
        step_size = current / pattern_sum(inner(direction, applied))
        solution = solution + widen(step_size) * direction
        residue = residue - widen(step_size) * applied
        if iteration + 1 < ITERS:
            precond = residue / diagonal
            following = pattern_sum(inner(residue, precond))
            direction = precond + widen(following / current) * direction
            current = following
    return solution


def per_device(conductivity, warm_forward, warm_adjoint, electrodes, patterns, observed):
    plane_count, pattern_count, row_count, column_count = warm_forward.shape
    position = lax.axis_index("vox")
    layers = lax.axis_size("vox")
    strength = 2.0 * math.sqrt(layers * plane_count * row_count * column_count)
    data_weight = 0.1 * strength
    lower_open = (position > 0).astype(jnp.float32)
    upper_open = (position < layers - 1).astype(jnp.float32)
    padded_sigma = extended(conductivity, (("vox", 0),), 1)
    face_mask = jnp.concatenate(
        [lower_open[None], jnp.ones((plane_count - 1,), jnp.float32), upper_open[None]]
    )
    depth_faces = 0.5 * (padded_sigma[1:] + padded_sigma[:-1]) * face_mask[:, None, None]
    row_faces = 0.5 * (conductivity[:, 1:] + conductivity[:, :-1])
    column_faces = 0.5 * (conductivity[:, :, 1:] + conductivity[:, :, :-1])
    coeffs = (depth_faces, row_faces, column_faces)
    diagonal = (
        leakage
        + (depth_faces[:-1] + depth_faces[1:])
        + both_sides(row_faces, 1)
        + both_sides(column_faces, 2)
    )
    diagonal = diagonal[:, None]
    electrode_ids = jnp.arange(electrodes.shape[0], dtype=jnp.int32)
    picked = jnp.sum(
        jnp.where(
            patterns[:, :, None] == electrode_ids[None, None, :], electrodes[None, None, :], 0
        ),
        axis=2,
    )
    offset = position * (plane_count * row_count * column_count)
    local_cell = picked - offset
    grid_shape = (plane_count, 1, row_count, column_count)
    cell_index = (
        lax.broadcasted_iota(jnp.int32, grid_shape, 0) * row_count
        + lax.broadcasted_iota(jnp.int32, grid_shape, 2)
    ) * column_count + lax.broadcasted_iota(jnp.int32, grid_shape, 3)

    def marker(which_one):
        return (cell_index == local_cell[:, which_one][None, :, None, None]).astype(jnp.float32)

    forward = solve_pattern(strength * (marker(0) - marker(1)), warm_forward, coeffs, diagonal)
    probe_weights = marker(2) - marker(3)
    predicted = lax.psum(inner(probe_weights, forward), "vox")
    misfit = predicted - observed
    adjoint = solve_pattern(
        widen(data_weight * misfit) * probe_weights, warm_adjoint, coeffs, diagonal
    )
    stacked = jnp.concatenate([forward, adjoint], axis=1)
    padded_pair = extended(stacked, (("vox", 0),), 1)
    padded_forward = padded_pair[:, :pattern_count]
    padded_adjoint = padded_pair[:, pattern_count:]
    depth_products = jnp.sum(
        (padded_forward[1:] - padded_forward[:-1]) * (padded_adjoint[1:] - padded_adjoint[:-1]),
        axis=1,
    )
    depth_products = depth_products * face_mask[:, None, None]
    grad_depth = depth_products[:-1] + depth_products[1:]
    row_products = jnp.sum(
        (forward[:, :, 1:] - forward[:, :, :-1]) * (adjoint[:, :, 1:] - adjoint[:, :, :-1]), axis=1
    )
    column_products = jnp.sum(
        (forward[:, :, :, 1:] - forward[:, :, :, :-1])
        * (adjoint[:, :, :, 1:] - adjoint[:, :, :, :-1]),
        axis=1,
    )
    local_gradient = -0.5 * (
        grad_depth + both_sides(row_products, 1) + both_sides(column_products, 2)
    )
    gradient = lax.psum(local_gradient, "pat")
    return (gradient, predicted)


def solution(mesh):
    in_specs = (
        P("vox", None, None),
        P("vox", "pat", None, None),
        P("vox", "pat", None, None),
        P(),
        P("pat", None),
        P("pat"),
    )
    out_specs = (P("vox", None, None), P("pat"))
    return jax.shard_map(
        per_device, mesh=mesh, in_specs=in_specs, out_specs=out_specs, check_vma=False
    )
```

profile of v0, /device:TPU:0, one launch (start us, length us, event | category | flops | bytes accessed | tf_op | source)
XLA Modules:
  0.0 282.5 jit_solution(13601715273596078150)
XLA Ops:
  8.2 1.3 collective-permute-start
  9.5 3.0 %collective-permute-start.1 = (f32[1,128,128]{2,1,0:T(8,128)S(1)}, f32[1,128,128]{2,1,0:T(8,128)S(1)}, u32[]{:S(2)}, u32[]{:S(2)}) collective-permute-start(f32[1,128,128]{2,1,0:T(8,128)S(1)} %get-tuple-element.42), channel_id=1, source_target_pairs={{0,1},{1,2},{2,3},{3,4},{4,5},{5,6},{6,7},{8,9},{9,10},{10,11},{11... | collective-permute-start | bytes 196616 | tf_op jit(solution)/shard_map/ppermute | solution.py:16
  12.5 2.1 fusion.61
  14.6 1.4 collective-permute-start.2
  16.1 5.9 %collective-permute-start.3 = (f32[1,8,128,128]{3,2,1,0:T(8,128)S(1)}, f32[1,8,128,128]{3,2,1,0:T(8,128)}, u32[]{:S(2)}, u32[]{:S(2)}) collective-permute-start(f32[1,8,128,128]{3,2,1,0:T(8,128)S(1)} %get-tuple-element.32), channel_id=1, source_target_pairs={{0,1},{1,2},{2,3},{3,4},{4,5},{5,6},{6,7},{8,9},{9,10},{10,11},{11... | collective-permute-start | bytes 1572872 | tf_op jit(solution)/shard_map/ppermute | solution.py:16
  23.1 3.7 %collective-permute-start.9 = (f32[1,8,128,128]{3,2,1,0:T(8,128)}, f32[1,8,128,128]{3,2,1,0:T(8,128)}, u32[]{:S(2)}, u32[]{:S(2)}) collective-permute-start(f32[1,8,128,128]{3,2,1,0:T(8,128)} %get-tuple-element.34), channel_id=1, source_target_pairs={{0,1},{1,2},{2,3},{3,4},{4,5},{5,6},{6,7},{8,9},{9,10},{10,11},{11... | collective-permute-start | bytes 1572872 | tf_op jit(solution)/shard_map/ppermute | solution.py:16
  28.7 1.4 fusion.2
  31.0 1.4 collective-permute-start.4
  32.5 3.3 %collective-permute-start.5 = (f32[1,8,128,128]{3,2,1,0:T(8,128)S(1)}, f32[1,8,128,128]{3,2,1,0:T(8,128)S(1)}, u32[]{:S(2)}, u32[]{:S(2)}) collective-permute-start(f32[1,8,128,128]{3,2,1,0:T(8,128)S(1)} %get-tuple-element.30), channel_id=1, source_target_pairs={{0,1},{1,2},{2,3},{3,4},{4,5},{5,6},{6,7},{8,9},{9,10},{10,11},{11... | collective-permute-start | bytes 1572872 | tf_op jit(solution)/shard_map/ppermute | solution.py:16
  37.5 1.7 multiply_reduce_fusion.5
  39.2 27.2 %all-reduce.33 = (f32[8]{0:T(128)S(1)}, f32[8]{0:T(128)S(1)}) all-reduce(f32[8]{0:T(128)S(1)} %get-tuple-element.5, f32[8]{0:T(128)S(1)} %get-tuple-element.4), channel_id=1, replica_groups=mesh['pat'=4,'vox'=8] {'vox'}, use_global_device_ids=true, to_apply=%region_2.3 | all-reduce | flops 16 | bytes 128 | tf_op jit(solution)/shard_map/psum | solution.py:61
  66.5 1.6 multiply_reduce_fusion.4
  69.3 15.8 %psum.72 = f32[8]{0:T(128)S(1)} all-reduce(f32[8]{0:T(128)S(1)} %multiply_reduce_fusion.4), channel_id=1, replica_groups=mesh['pat'=4,'vox'=8] {'vox'}, use_global_device_ids=true, to_apply=%region_6.7 | all-reduce | flops 8 | bytes 64 | tf_op jit(solution)/shard_map/psum | solution.py:61
  85.2 1.8 multiply_add_fusion.3
  87.1 1.3 collective-permute-start.6
  88.4 3.2 %collective-permute-start.7 = (f32[1,8,128,128]{3,2,1,0:T(8,128)S(1)}, f32[1,8,128,128]{3,2,1,0:T(8,128)S(1)}, u32[]{:S(2)}, u32[]{:S(2)}) collective-permute-start(f32[1,8,128,128]{3,2,1,0:T(8,128)S(1)} %get-tuple-element.28), channel_id=1, source_target_pairs={{0,1},{1,2},{2,3},{3,4},{4,5},{5,6},{6,7},{8,9},{9,10},{10,11},{11... | collective-permute-start | bytes 1572872 | tf_op jit(solution)/shard_map/ppermute | solution.py:16
  91.6 1.6 fusion.29
  94.5 2.8 fusion.4
  98.0 20.6 %psum.73 = f32[8]{0:T(128)S(1)} all-reduce(f32[8]{0:T(128)S(1)} %fusion.35), channel_id=1, replica_groups=mesh['pat'=4,'vox'=8] {'vox'}, use_global_device_ids=true, to_apply=%region_8.9 | all-reduce | flops 8 | bytes 64 | tf_op jit(solution)/shard_map/psum | solution.py:61
  118.6 2.8 multiply_reduce_fusion.3
  121.4 12.4 %psum.74 = f32[8]{0:T(128)S(1)} all-reduce(f32[8]{0:T(128)S(1)} %get-tuple-element.15), channel_id=1, replica_groups=mesh['pat'=4,'vox'=8] {'vox'}, use_global_device_ids=true, to_apply=%region_10.11 | all-reduce | flops 8 | bytes 64 | tf_op jit(solution)/shard_map/psum | solution.py:126
  133.9 3.7 %broadcast_divide_fusion = (f32[2,8,128,128]{3,2,1,0:T(8,128)S(1)}, f32[2,8,128,128]{3,2,1,0:T(8,128)S(1)}) fusion(f32[2,128,128]{2,1,0:T(8,128)S(1)} %fusion.51, f32[2,8,128,127]{3,2,1,0:T(8,128)} %get-tuple-element.41, f32[2,8,127,128]{3,2,1,0:T(8,128)} %get-tuple-element.39, f32[3,8,128,128]{3,2,1,0:T(8,128)} %get-tuple-element.37, ...), kind=kLoop, calls=%fused_computation.94 | loop fusion | flops 3932160 | bytes 7585888 | tf_op jit(solution)/shard_map/div | solution.py:67
  137.7 1.3 collective-permute-start.10
  139.0 3.2 %collective-permute-start.11 = (f32[1,8,128,128]{3,2,1,0:T(8,128)S(1)}, f32[1,8,128,128]{3,2,1,0:T(8,128)S(1)}, u32[]{:S(2)}, u32[]{:S(2)}) collective-permute-start(f32[1,8,128,128]{3,2,1,0:T(8,128)S(1)} %get-tuple-element.26), channel_id=1, source_target_pairs={{0,1},{1,2},{2,3},{3,4},{4,5},{5,6},{6,7},{8,9},{9,10},{10,11},{11... | collective-permute-start | bytes 1572872 | tf_op jit(solution)/shard_map/ppermute | solution.py:16
  144.7 20.3 %all-reduce.32 = (f32[8]{0:T(128)S(1)}, f32[8]{0:T(128)S(1)}) all-reduce(f32[8]{0:T(128)S(1)} %get-tuple-element.3, f32[8]{0:T(128)S(1)} %get-tuple-element.2), channel_id=1, replica_groups=mesh['pat'=4,'vox'=8] {'vox'}, use_global_device_ids=true, to_apply=%region_12.13 | all-reduce | flops 16 | bytes 128 | tf_op jit(solution)/shard_map/psum | solution.py:61
  165.4 12.6 %psum.77 = f32[8]{0:T(128)S(1)} all-reduce(f32[8]{0:T(128)S(1)} %multiply_reduce_fusion), channel_id=1, replica_groups=mesh['pat'=4,'vox'=8] {'vox'}, use_global_device_ids=true, to_apply=%region_16.17 | all-reduce | flops 8 | bytes 64 | tf_op jit(solution)/shard_map/psum | solution.py:61
  178.0 1.5 multiply_add_fusion.1
  180.9 3.2 %collective-permute-start.13 = (f32[1,8,128,128]{3,2,1,0:T(8,128)S(1)}, f32[1,8,128,128]{3,2,1,0:T(8,128)S(1)}, u32[]{:S(2)}, u32[]{:S(2)}) collective-permute-start(f32[1,8,128,128]{3,2,1,0:T(8,128)S(1)} %get-tuple-element.24), channel_id=1, source_target_pairs={{0,1},{1,2},{2,3},{3,4},{4,5},{5,6},{6,7},{8,9},{9,10},{10,11},{11... | collective-permute-start | bytes 1572872 | tf_op jit(solution)/shard_map/ppermute | solution.py:16
  186.5 20.7 %psum.78 = f32[8]{0:T(128)S(1)} all-reduce(f32[8]{0:T(128)S(1)} %fusion.19), channel_id=1, replica_groups=mesh['pat'=4,'vox'=8] {'vox'}, use_global_device_ids=true, to_apply=%region_18.19 | all-reduce | flops 8 | bytes 64 | tf_op jit(solution)/shard_map/psum | solution.py:61
  210.0 3.1 %collective-permute-start.15 = (f32[1,16,128,128]{3,2,1,0:T(8,128)S(1)}, f32[1,16,128,128]{3,2,1,0:T(8,128)S(1)}, u32[]{:S(2)}, u32[]{:S(2)}) collective-permute-start(f32[1,16,128,128]{3,2,1,0:T(8,128)S(1)} %get-tuple-element.23), channel_id=1, source_target_pairs={{0,1},{1,2},{2,3},{3,4},{4,5},{5,6},{6,7},{8,9},{9,10},{10,11},{11... | collective-permute-start | bytes 3145736 | tf_op jit(solution)/shard_map/ppermute | solution.py:16
  217.7 56.4 %all-reduce.36.cloned.1.call-done = f32[2,128,128]{2,1,0:T(8,128)} async-done(((f32[2,128,128]{2,1,0:T(8,128)}), f32[2,128,128]{2,1,0:T(8,128)}) %all-reduce.36.cloned.1.call-update) | async-done | bytes 131088 | tf_op jit(solution)/shard_map/psum | solution.py:152
  274.0 1.6 copy.10
  (112 shorter events, 23.7 us)
Async XLA Ops:
  7.2 14.8 %copy-start = (f32[2,8,128,128]{3,2,1,0:T(8,128)S(1)}, f32[2,8,128,128]{3,2,1,0:T(8,128)}, u32[]{:S(2)}) copy-start(f32[2,8,128,128]{3,2,1,0:T(8,128)} %param.8) | copy-start | bytes 3145732
  7.2 266.9 %all-reduce.36.cloned.1.call-start = ((), (), s32[]{:S(2)}) async-start(), calls=%async_computation | async-start | bytes 262144 | tf_op jit(solution)/shard_map/psum | solution.py:152
  8.2 20.3 %collective-permute-start = (f32[1,128,128]{2,1,0:T(8,128)S(1)}, f32[1,128,128]{2,1,0:T(8,128)S(1)}, u32[]{:S(2)}, u32[]{:S(2)}) collective-permute-start(f32[1,128,128]{2,1,0:T(8,128)S(1)} %get-tuple-element.43), channel_id=1, source_target_pairs={{1,0},{2,1},{3,2},{4,3},{5,4},{6,5},{7,6},{9,8},{10,9},{11,10},{12... | collective-permute-start | bytes 196616 | tf_op jit(solution)/shard_map/ppermute | solution.py:19
  9.5 19.0 %collective-permute-start.1 = (f32[1,128,128]{2,1,0:T(8,128)S(1)}, f32[1,128,128]{2,1,0:T(8,128)S(1)}, u32[]{:S(2)}, u32[]{:S(2)}) collective-permute-start(f32[1,128,128]{2,1,0:T(8,128)S(1)} %get-tuple-element.42), channel_id=1, source_target_pairs={{0,1},{1,2},{2,3},{3,4},{4,5},{5,6},{6,7},{8,9},{9,10},{10,11},{11... | collective-permute-start | bytes 196616 | tf_op jit(solution)/shard_map/ppermute | solution.py:16
  14.6 12.1 %copy-start.15 = (f32[2,128,128]{2,1,0:T(8,128)S(1)}, f32[2,128,128]{2,1,0:T(8,128)}, u32[]{:S(2)}) copy-start(f32[2,128,128]{2,1,0:T(8,128)} %param.6) | copy-start | bytes 393220
  14.6 13.0 %copy-start.17 = (s32[8,4]{0,1:T(4,128)S(1)}, s32[8,4]{0,1:T(4,128)}, u32[]{:S(2)}) copy-start(s32[8,4]{0,1:T(4,128)} %param.10) | copy-start | bytes 388
  14.6 13.0 %copy-start.18 = (s32[128]{0:T(128)S(1)}, s32[128]{0:T(128)}, u32[]{:S(2)}) copy-start(s32[128]{0:T(128)} %param.9) | copy-start | bytes 1540
  14.6 13.3 %copy-start.1 = (f32[2,8,128,128]{3,2,1,0:T(8,128)S(1)}, f32[2,8,128,128]{3,2,1,0:T(8,128)}, u32[]{:S(2)}) copy-start(f32[2,8,128,128]{3,2,1,0:T(8,128)} %param.7) | copy-start | bytes 3145732
  14.6 14.1 %collective-permute-start.2 = (f32[1,8,128,128]{3,2,1,0:T(8,128)}, f32[1,8,128,128]{3,2,1,0:T(8,128)}, u32[]{:S(2)}, u32[]{:S(2)}) collective-permute-start(f32[1,8,128,128]{3,2,1,0:T(8,128)} %get-tuple-element.33), channel_id=1, source_target_pairs={{1,0},{2,1},{3,2},{4,3},{5,4},{6,5},{7,6},{9,8},{10,9},{11,10},{12... | collective-permute-start | bytes 1572872 | tf_op jit(solution)/shard_map/ppermute | solution.py:19
  16.1 12.7 %collective-permute-start.3 = (f32[1,8,128,128]{3,2,1,0:T(8,128)S(1)}, f32[1,8,128,128]{3,2,1,0:T(8,128)}, u32[]{:S(2)}, u32[]{:S(2)}) collective-permute-start(f32[1,8,128,128]{3,2,1,0:T(8,128)S(1)} %get-tuple-element.32), channel_id=1, source_target_pairs={{0,1},{1,2},{2,3},{3,4},{4,5},{5,6},{6,7},{8,9},{9,10},{10,11},{11... | collective-permute-start | bytes 1572872 | tf_op jit(solution)/shard_map/ppermute | solution.py:16
  23.1 71.4 %collective-permute-start.9 = (f32[1,8,128,128]{3,2,1,0:T(8,128)}, f32[1,8,128,128]{3,2,1,0:T(8,128)}, u32[]{:S(2)}, u32[]{:S(2)}) collective-permute-start(f32[1,8,128,128]{3,2,1,0:T(8,128)} %get-tuple-element.34), channel_id=1, source_target_pairs={{0,1},{1,2},{2,3},{3,4},{4,5},{5,6},{6,7},{8,9},{9,10},{10,11},{11... | collective-permute-start | bytes 1572872 | tf_op jit(solution)/shard_map/ppermute | solution.py:16
  30.9 35.5 %copy-start.3 = (f32[2,8,128,128]{3,2,1,0:T(8,128)}, f32[2,8,128,128]{3,2,1,0:T(8,128)S(1)}, u32[]{:S(2)}) copy-start(f32[2,8,128,128]{3,2,1,0:T(8,128)S(1)} %get-tuple-element.19) | copy-start | bytes 3145732
  31.0 4.9 %copy-start.11 = (f32[2,128,127]{2,1,0:T(8,128)S(1)}, f32[2,128,127]{2,1,0:T(8,128)}, u32[]{:S(2)}) copy-start(f32[2,128,127]{2,1,0:T(8,128)} %copy-done.10) | copy-start | bytes 390148
  31.0 5.3 %collective-permute-start.4 = (f32[1,8,128,128]{3,2,1,0:T(8,128)S(1)}, f32[1,8,128,128]{3,2,1,0:T(8,128)S(1)}, u32[]{:S(2)}, u32[]{:S(2)}) collective-permute-start(f32[1,8,128,128]{3,2,1,0:T(8,128)S(1)} %get-tuple-element.31), channel_id=1, source_target_pairs={{1,0},{2,1},{3,2},{4,3},{5,4},{6,5},{7,6},{9,8},{10,9},{11,10},{12... | collective-permute-start | bytes 1572872 | tf_op jit(solution)/shard_map/ppermute | solution.py:19
  32.5 3.7 %copy-start.6 = (f32[2,127,128]{2,1,0:T(8,128)S(1)}, f32[2,127,128]{2,1,0:T(8,128)}, u32[]{:S(2)}) copy-start(f32[2,127,128]{2,1,0:T(8,128)} %copy-done.5) | copy-start | bytes 390148
  32.5 4.8 %collective-permute-start.5 = (f32[1,8,128,128]{3,2,1,0:T(8,128)S(1)}, f32[1,8,128,128]{3,2,1,0:T(8,128)S(1)}, u32[]{:S(2)}, u32[]{:S(2)}) collective-permute-start(f32[1,8,128,128]{3,2,1,0:T(8,128)S(1)} %get-tuple-element.30), channel_id=1, source_target_pairs={{0,1},{1,2},{2,3},{3,4},{4,5},{5,6},{6,7},{8,9},{9,10},{10,11},{11... | collective-permute-start | bytes 1572872 | tf_op jit(solution)/shard_map/ppermute | solution.py:16
  68.0 26.5 %collective-permute-start.8 = (f32[1,8,128,128]{3,2,1,0:T(8,128)}, f32[1,8,128,128]{3,2,1,0:T(8,128)}, u32[]{:S(2)}, u32[]{:S(2)}) collective-permute-start(f32[1,8,128,128]{3,2,1,0:T(8,128)} %get-tuple-element.35), channel_id=1, source_target_pairs={{1,0},{2,1},{3,2},{4,3},{5,4},{6,5},{7,6},{9,8},{10,9},{11,10},{12... | collective-permute-start | bytes 1572872 | tf_op jit(solution)/shard_map/ppermute | solution.py:19
  87.0 4.6 %copy-start.12 = (f32[2,128,127]{2,1,0:T(8,128)S(1)}, f32[2,128,127]{2,1,0:T(8,128)}, u32[]{:S(2)}) copy-start(f32[2,128,127]{2,1,0:T(8,128)} %copy-done.10) | copy-start | bytes 390148
  87.1 7.4 %collective-permute-start.6 = (f32[1,8,128,128]{3,2,1,0:T(8,128)S(1)}, f32[1,8,128,128]{3,2,1,0:T(8,128)S(1)}, u32[]{:S(2)}, u32[]{:S(2)}) collective-permute-start(f32[1,8,128,128]{3,2,1,0:T(8,128)S(1)} %get-tuple-element.29), channel_id=1, source_target_pairs={{1,0},{2,1},{3,2},{4,3},{5,4},{6,5},{7,6},{9,8},{10,9},{11,10},{12... | collective-permute-start | bytes 1572872 | tf_op jit(solution)/shard_map/ppermute | solution.py:19
  88.4 4.8 %copy-start.7 = (f32[2,127,128]{2,1,0:T(8,128)S(1)}, f32[2,127,128]{2,1,0:T(8,128)}, u32[]{:S(2)}) copy-start(f32[2,127,128]{2,1,0:T(8,128)} %copy-done.5) | copy-start | bytes 390148
  88.4 6.1 %collective-permute-start.7 = (f32[1,8,128,128]{3,2,1,0:T(8,128)S(1)}, f32[1,8,128,128]{3,2,1,0:T(8,128)S(1)}, u32[]{:S(2)}, u32[]{:S(2)}) collective-permute-start(f32[1,8,128,128]{3,2,1,0:T(8,128)S(1)} %get-tuple-element.28), channel_id=1, source_target_pairs={{0,1},{1,2},{2,3},{3,4},{4,5},{5,6},{6,7},{8,9},{9,10},{10,11},{11... | collective-permute-start | bytes 1572872 | tf_op jit(solution)/shard_map/ppermute | solution.py:16
  118.6 15.3 %copy-start.19 = (f32[8]{0:T(128)S(1)}, f32[8]{0:T(128)}, u32[]{:S(2)}) copy-start(f32[8]{0:T(128)} %param.11) | copy-start | bytes 100
  133.9 3.8 %copy-start.20 = (f32[8]{0:T(128)}, f32[8]{0:T(128)S(1)}, u32[]{:S(2)}) copy-start(f32[8]{0:T(128)S(1)} %psum.74) | copy-start | bytes 100
  137.6 4.6 %copy-start.13 = (f32[2,128,127]{2,1,0:T(8,128)S(1)}, f32[2,128,127]{2,1,0:T(8,128)}, u32[]{:S(2)}) copy-start(f32[2,128,127]{2,1,0:T(8,128)} %copy-done.10) | copy-start | bytes 390148
  137.7 5.0 %collective-permute-start.10 = (f32[1,8,128,128]{3,2,1,0:T(8,128)S(1)}, f32[1,8,128,128]{3,2,1,0:T(8,128)S(1)}, u32[]{:S(2)}, u32[]{:S(2)}) collective-permute-start(f32[1,8,128,128]{3,2,1,0:T(8,128)S(1)} %get-tuple-element.27), channel_id=1, source_target_pairs={{1,0},{2,1},{3,2},{4,3},{5,4},{6,5},{7,6},{9,8},{10,9},{11,10},{12... | collective-permute-start | bytes 1572872 | tf_op jit(solution)/shard_map/ppermute | solution.py:19
  139.0 4.7 %collective-permute-start.11 = (f32[1,8,128,128]{3,2,1,0:T(8,128)S(1)}, f32[1,8,128,128]{3,2,1,0:T(8,128)S(1)}, u32[]{:S(2)}, u32[]{:S(2)}) collective-permute-start(f32[1,8,128,128]{3,2,1,0:T(8,128)S(1)} %get-tuple-element.26), channel_id=1, source_target_pairs={{0,1},{1,2},{2,3},{3,4},{4,5},{5,6},{6,7},{8,9},{9,10},{10,11},{11... | collective-permute-start | bytes 1572872 | tf_op jit(solution)/shard_map/ppermute | solution.py:16
  144.7 33.3 %copy-start.4 = (f32[2,8,128,128]{3,2,1,0:T(8,128)}, f32[2,8,128,128]{3,2,1,0:T(8,128)S(1)}, u32[]{:S(2)}) copy-start(f32[2,8,128,128]{3,2,1,0:T(8,128)S(1)} %get-tuple-element.12) | copy-start | bytes 3145732
  179.5 4.6 %copy-start.14 = (f32[2,128,127]{2,1,0:T(8,128)S(1)}, f32[2,128,127]{2,1,0:T(8,128)}, u32[]{:S(2)}) copy-start(f32[2,128,127]{2,1,0:T(8,128)} %copy-done.10) | copy-start | bytes 390148
  179.6 5.0 %collective-permute-start.12 = (f32[1,8,128,128]{3,2,1,0:T(8,128)S(1)}, f32[1,8,128,128]{3,2,1,0:T(8,128)S(1)}, u32[]{:S(2)}, u32[]{:S(2)}) collective-permute-start(f32[1,8,128,128]{3,2,1,0:T(8,128)S(1)} %get-tuple-element.25), channel_id=1, source_target_pairs={{1,0},{2,1},{3,2},{4,3},{5,4},{6,5},{7,6},{9,8},{10,9},{11,10},{12... | collective-permute-start | bytes 1572872 | tf_op jit(solution)/shard_map/ppermute | solution.py:19
  180.9 4.7 %collective-permute-start.13 = (f32[1,8,128,128]{3,2,1,0:T(8,128)S(1)}, f32[1,8,128,128]{3,2,1,0:T(8,128)S(1)}, u32[]{:S(2)}, u32[]{:S(2)}) collective-permute-start(f32[1,8,128,128]{3,2,1,0:T(8,128)S(1)} %get-tuple-element.24), channel_id=1, source_target_pairs={{0,1},{1,2},{2,3},{3,4},{4,5},{5,6},{6,7},{8,9},{9,10},{10,11},{11... | collective-permute-start | bytes 1572872 | tf_op jit(solution)/shard_map/ppermute | solution.py:16
  208.7 5.3 %collective-permute-start.14 = (f32[1,16,128,128]{3,2,1,0:T(8,128)S(1)}, f32[1,16,128,128]{3,2,1,0:T(8,128)S(1)}, u32[]{:S(2)}, u32[]{:S(2)}) collective-permute-start(f32[1,16,128,128]{3,2,1,0:T(8,128)S(1)} %get-tuple-element.22), channel_id=1, source_target_pairs={{1,0},{2,1},{3,2},{4,3},{5,4},{6,5},{7,6},{9,8},{10,9},{11,10},{12... | collective-permute-start | bytes 3145736 | tf_op jit(solution)/shard_map/ppermute | solution.py:19
  210.0 5.3 %collective-permute-start.15 = (f32[1,16,128,128]{3,2,1,0:T(8,128)S(1)}, f32[1,16,128,128]{3,2,1,0:T(8,128)S(1)}, u32[]{:S(2)}, u32[]{:S(2)}) collective-permute-start(f32[1,16,128,128]{3,2,1,0:T(8,128)S(1)} %get-tuple-element.23), channel_id=1, source_target_pairs={{0,1},{1,2},{2,3},{3,4},{4,5},{5,6},{6,7},{8,9},{9,10},{10,11},{11... | collective-permute-start | bytes 3145736 | tf_op jit(solution)/shard_map/ppermute | solution.py:16
  (6 other events, 13.3 us)
Sparse Core Ops, SparseCore 0:
  217.8 56.2 all-reduce.35
where the time goes:
time: 283 us; the launch traced here: 282 us
  blocking collectives  130 us (46%)
  waiting for transfers between devices  60.6 us (21%)
  starting transfers between devices  39.3 us (14%)
  other arithmetic  31.2 us (11%)
  between operations  14.7 us (5%)
  local copies, waits for them, and re-layouts  7.01 us (2%)
    psum x6, blocking collectives, pattern_sum(): return lax.psum(local_terms, 'vox')  117 us
    psum x1, waiting for transfers between devices, per_device(): gradient = lax.psum(local_gradient, 'pat')  56.4 us
    ppermute x8, starting transfers between devices, extended(): lax.ppermute(lax.slice_in_dim(block, block.shape[dim] - width, None, axis...  28.6 us
    psum x1, blocking collectives, per_device(): predicted = lax.psum(inner(probe_weights, forward), 'vox')  12.4 us
    ppermute x8, starting transfers between devices, extended(): lax.ppermute(lax.slice_in_dim(block, 0, width, axis=dim), axis, backward)  10.6 us
    reduce_sum x7, other arithmetic, inner(): return jnp.sum(left_factor * right_factor, axis=(0, 2, 3))  8.68 us
  transfers between devices with their start and end apart: 17, of which 5 were waited for; matrix products, arithmetic and copies ran while one was open for 6% of the time, Pallas kernels for 0%

commit v1 on v0

--- a/solution.py
+++ b/solution.py
@@ -149,7 +149,9 @@
     local_gradient = -0.5 * (
         grad_depth + both_sides(row_products, 1) + both_sides(column_products, 2)
     )
-    gradient = lax.psum(local_gradient, "pat")
+    gradient = local_gradient
+    for hop in (1, 2):
+        gradient = gradient + lax.ppermute(gradient, "pat", [(dev, dev ^ hop) for dev in range(4)])
     return (gradient, predicted)
 
 

time: 283 us -> 244 us (0.86)
  the two profiles are of different devices: /device:TPU:0 before, /device:TPU:4 now
where the time goes in v1:
time: 244 us; the launch traced here: 243 us
  blocking collectives  89.3 us (37%)
  waiting for transfers between devices  72.6 us (30%)
  starting transfers between devices  43.5 us (18%)
  other arithmetic  31.2 us (13%)
  local copies, waits for them, and re-layouts  5.44 us (2%)
    psum x6, blocking collectives, pattern_sum(): return lax.psum(local_terms, 'vox')  77.5 us
    ppermute x8, waiting for transfers between devices, extended(): lax.ppermute(lax.slice_in_dim(block, 0, width, axis=dim), axis, backward)  47.7 us
    ppermute x8, starting transfers between devices, extended(): lax.ppermute(lax.slice_in_dim(block, 0, width, axis=dim), axis, backward)  21.1 us
    ppermute x8, starting transfers between devices, extended(): lax.ppermute(lax.slice_in_dim(block, block.shape[dim] - width, None, axis...  17.6 us
    ppermute x8, waiting for transfers between devices, extended(): lax.ppermute(lax.slice_in_dim(block, block.shape[dim] - width, None, axis...  17.1 us
    psum x1, blocking collectives, per_device(): predicted = lax.psum(inner(probe_weights, forward), 'vox')  11.8 us
    reduce_sum x7, other arithmetic, inner(): return jnp.sum(left_factor * right_factor, axis=(0, 2, 3))  8.68 us
    ppermute x2, waiting for transfers between devices, per_device(): lax.ppermute(gradient, 'pat', [(dev, dev ^ hop) for dev in range(4)])  7.74 us
  transfers between devices with their start and end apart: 18, of which 14 were waited for; matrix products, arithmetic and copies ran while one was open for 7% of the time, Pallas kernels for 0%

profile of v1, /device:TPU:4, one launch (start us, length us, event | category | flops | bytes accessed | tf_op | source)
XLA Modules:
  0.0 243.4 jit_solution(13638856616867834874)
XLA Ops:
  1.6 2.8 %collective-permute-start = (f32[1,128,128]{2,1,0:T(8,128)S(1)}, f32[1,128,128]{2,1,0:T(8,128)S(1)}, u32[]{:S(2)}, u32[]{:S(2)}) collective-permute-start(f32[1,128,128]{2,1,0:T(8,128)S(1)} %get-tuple-element.43), channel_id=1, source_target_pairs={{1,0},{2,1},{3,2},{4,3},{5,4},{6,5},{7,6},{9,8},{10,9},{11,10},{12... | collective-permute-start | bytes 196616 | tf_op jit(solution)/shard_map/ppermute | solution.py:19
  6.3 2.1 fusion.61
  8.4 4.7 %collective-permute-start.2 = (f32[1,8,128,128]{3,2,1,0:T(8,128)}, f32[1,8,128,128]{3,2,1,0:T(8,128)}, u32[]{:S(2)}, u32[]{:S(2)}) collective-permute-start(f32[1,8,128,128]{3,2,1,0:T(8,128)} %get-tuple-element.33), channel_id=1, source_target_pairs={{1,0},{2,1},{3,2},{4,3},{5,4},{6,5},{7,6},{9,8},{10,9},{11,10},{12... | collective-permute-start | bytes 1572872 | tf_op jit(solution)/shard_map/ppermute | solution.py:19
  20.0 4.8 %collective-permute-done.2 = f32[1,8,128,128]{3,2,1,0:T(8,128)} collective-permute-done((f32[1,8,128,128]{3,2,1,0:T(8,128)}, f32[1,8,128,128]{3,2,1,0:T(8,128)}, u32[]{:S(2)}, u32[]{:S(2)}) %collective-permute-start.2) | collective-permute-done | bytes 524320 | tf_op jit(solution)/shard_map/ppermute | solution.py:19
  28.1 3.9 %collective-permute-start.4 = (f32[1,8,128,128]{3,2,1,0:T(8,128)S(1)}, f32[1,8,128,128]{3,2,1,0:T(8,128)S(1)}, u32[]{:S(2)}, u32[]{:S(2)}) collective-permute-start(f32[1,8,128,128]{3,2,1,0:T(8,128)S(1)} %get-tuple-element.31), channel_id=1, source_target_pairs={{1,0},{2,1},{3,2},{4,3},{5,4},{6,5},{7,6},{9,8},{10,9},{11,10},{12... | collective-permute-start | bytes 1572872 | tf_op jit(solution)/shard_map/ppermute | solution.py:19
  34.6 7.7 %collective-permute-done.4 = f32[1,8,128,128]{3,2,1,0:T(8,128)S(1)} collective-permute-done((f32[1,8,128,128]{3,2,1,0:T(8,128)S(1)}, f32[1,8,128,128]{3,2,1,0:T(8,128)S(1)}, u32[]{:S(2)}, u32[]{:S(2)}) %collective-permute-start.4) | collective-permute-done | bytes 524320 | tf_op jit(solution)/shard_map/ppermute | solution.py:19
  45.4 13.3 %all-reduce.33 = (f32[8]{0:T(128)S(1)}, f32[8]{0:T(128)S(1)}) all-reduce(f32[8]{0:T(128)S(1)} %get-tuple-element.5, f32[8]{0:T(128)S(1)} %get-tuple-element.4), channel_id=1, replica_groups=mesh['pat'=4,'vox'=8] {'vox'}, use_global_device_ids=true, to_apply=%region_2.3 | all-reduce | flops 16 | bytes 128 | tf_op jit(solution)/shard_map/psum | solution.py:61
  62.2 16.4 %psum.65 = f32[8]{0:T(128)S(1)} all-reduce(f32[8]{0:T(128)S(1)} %multiply_reduce_fusion.4), channel_id=1, replica_groups=mesh['pat'=4,'vox'=8] {'vox'}, use_global_device_ids=true, to_apply=%region_6.7 | all-reduce | flops 8 | bytes 64 | tf_op jit(solution)/shard_map/psum | solution.py:61
  82.5 2.5 %collective-permute-start.7 = (f32[1,8,128,128]{3,2,1,0:T(8,128)S(1)}, f32[1,8,128,128]{3,2,1,0:T(8,128)S(1)}, u32[]{:S(2)}, u32[]{:S(2)}) collective-permute-start(f32[1,8,128,128]{3,2,1,0:T(8,128)S(1)} %get-tuple-element.28), channel_id=1, source_target_pairs={{0,1},{1,2},{2,3},{3,4},{4,5},{5,6},{6,7},{8,9},{9,10},{10,11},{11... | collective-permute-start | bytes 1572872 | tf_op jit(solution)/shard_map/ppermute | solution.py:16
  88.0 5.0 %collective-permute-done.6 = f32[1,8,128,128]{3,2,1,0:T(8,128)S(1)} collective-permute-done((f32[1,8,128,128]{3,2,1,0:T(8,128)S(1)}, f32[1,8,128,128]{3,2,1,0:T(8,128)S(1)}, u32[]{:S(2)}, u32[]{:S(2)}) %collective-permute-start.6) | collective-permute-done | bytes 524320 | tf_op jit(solution)/shard_map/ppermute | solution.py:19
  92.9 2.1 collective-permute-done.7
  95.0 2.8 %fusion.4 = (f32[3,8,128,128]{3,2,1,0:T(8,128)S(1)}, f32[3,8,128,128]{3,2,1,0:T(8,128)}) fusion(f32[1,8,128,128]{3,2,1,0:T(8,128)S(1)} %collective-permute-done.6, f32[2,8,128,128]{3,2,1,0:T(8,128)S(1)} %multiply_add_fusion.3, f32[1,8,128,128]{3,2,1,0:T(8,128)S(1)} %collective-permute-done.7, f32[3,128,128]{2,1,0:T(8,128)S(1)} %fusion.45, ...), kind=kLoop, calls=%fused_computation.13 | loop fusion | flops 3145728 | bytes 7536640 | tf_op jit(solution)/shard_map/mul | solution.py:43
  98.5 12.5 %psum.66 = f32[8]{0:T(128)S(1)} all-reduce(f32[8]{0:T(128)S(1)} %fusion.35), channel_id=1, replica_groups=mesh['pat'=4,'vox'=8] {'vox'}, use_global_device_ids=true, to_apply=%region_8.9 | all-reduce | flops 8 | bytes 64 | tf_op jit(solution)/shard_map/psum | solution.py:61
  111.0 2.8 %multiply_reduce_fusion.3 = (f32[8]{0:T(128)S(1)}, f32[2,8,128,128]{3,2,1,0:T(8,128)}) fusion(s32[2,128,128]{2,1,0:T(8,128)} %iota_add_fusion, s32[8]{0:T(128)S(1)} %get-tuple-element.45, s32[8]{0:T(128)S(1)} %get-tuple-element.46, f32[2,8,128,128]{3,2,1,0:T(8,128)S(1)} %multiply_add_fusion.3, f32[8]{0:T(128)S(1)} %div.49, ...), kind=kLoop, calls=%fused_computation.84 | loop fusion | flops 3145720 | bytes 4456608 | tf_op jit(solution)/shard_map/reduce_sum | solution.py:53
  113.8 11.8 %psum.67 = f32[8]{0:T(128)S(1)} all-reduce(f32[8]{0:T(128)S(1)} %get-tuple-element.15), channel_id=1, replica_groups=mesh['pat'=4,'vox'=8] {'vox'}, use_global_device_ids=true, to_apply=%region_10.11 | all-reduce | flops 8 | bytes 64 | tf_op jit(solution)/shard_map/psum | solution.py:126
  125.6 3.7 %broadcast_divide_fusion = (f32[2,8,128,128]{3,2,1,0:T(8,128)S(1)}, f32[2,8,128,128]{3,2,1,0:T(8,128)S(1)}) fusion(f32[2,128,128]{2,1,0:T(8,128)S(1)} %fusion.51, f32[2,8,128,127]{3,2,1,0:T(8,128)} %get-tuple-element.41, f32[2,8,127,128]{3,2,1,0:T(8,128)} %get-tuple-element.39, f32[3,8,128,128]{3,2,1,0:T(8,128)} %get-tuple-element.37, ...), kind=kLoop, calls=%fused_computation.94 | loop fusion | flops 3932160 | bytes 7585888 | tf_op jit(solution)/shard_map/div | solution.py:67
  131.4 2.5 %collective-permute-start.11 = (f32[1,8,128,128]{3,2,1,0:T(8,128)S(1)}, f32[1,8,128,128]{3,2,1,0:T(8,128)S(1)}, u32[]{:S(2)}, u32[]{:S(2)}) collective-permute-start(f32[1,8,128,128]{3,2,1,0:T(8,128)S(1)} %get-tuple-element.26), channel_id=1, source_target_pairs={{0,1},{1,2},{2,3},{3,4},{4,5},{5,6},{6,7},{8,9},{9,10},{10,11},{11... | collective-permute-start | bytes 1572872 | tf_op jit(solution)/shard_map/ppermute | solution.py:16
  134.5 6.2 %collective-permute-done.10 = f32[1,8,128,128]{3,2,1,0:T(8,128)S(1)} collective-permute-done((f32[1,8,128,128]{3,2,1,0:T(8,128)S(1)}, f32[1,8,128,128]{3,2,1,0:T(8,128)S(1)}, u32[]{:S(2)}, u32[]{:S(2)}) %collective-permute-start.10) | collective-permute-done | bytes 524320 | tf_op jit(solution)/shard_map/ppermute | solution.py:19
  140.7 4.4 %collective-permute-done.11 = f32[1,8,128,128]{3,2,1,0:T(8,128)S(1)} collective-permute-done((f32[1,8,128,128]{3,2,1,0:T(8,128)S(1)}, f32[1,8,128,128]{3,2,1,0:T(8,128)S(1)}, u32[]{:S(2)}, u32[]{:S(2)}) %collective-permute-start.11) | collective-permute-done | bytes 524320 | tf_op jit(solution)/shard_map/ppermute | solution.py:16
  146.1 11.8 %all-reduce.32 = (f32[8]{0:T(128)S(1)}, f32[8]{0:T(128)S(1)}) all-reduce(f32[8]{0:T(128)S(1)} %get-tuple-element.3, f32[8]{0:T(128)S(1)} %get-tuple-element.2), channel_id=1, replica_groups=mesh['pat'=4,'vox'=8] {'vox'}, use_global_device_ids=true, to_apply=%region_12.13 | all-reduce | flops 16 | bytes 128 | tf_op jit(solution)/shard_map/psum | solution.py:61
  158.3 11.8 %psum.70 = f32[8]{0:T(128)S(1)} all-reduce(f32[8]{0:T(128)S(1)} %multiply_reduce_fusion), channel_id=1, replica_groups=mesh['pat'=4,'vox'=8] {'vox'}, use_global_device_ids=true, to_apply=%region_16.17 | all-reduce | flops 8 | bytes 64 | tf_op jit(solution)/shard_map/psum | solution.py:61
  171.7 2.1 collective-permute-start.12
  173.8 2.4 collective-permute-start.13
  176.7 6.6 %collective-permute-done.12 = f32[1,8,128,128]{3,2,1,0:T(8,128)S(1)} collective-permute-done((f32[1,8,128,128]{3,2,1,0:T(8,128)S(1)}, f32[1,8,128,128]{3,2,1,0:T(8,128)S(1)}, u32[]{:S(2)}, u32[]{:S(2)}) %collective-permute-start.12) | collective-permute-done | bytes 524320 | tf_op jit(solution)/shard_map/ppermute | solution.py:19
  183.3 3.5 %collective-permute-done.13 = f32[1,8,128,128]{3,2,1,0:T(8,128)S(1)} collective-permute-done((f32[1,8,128,128]{3,2,1,0:T(8,128)S(1)}, f32[1,8,128,128]{3,2,1,0:T(8,128)S(1)}, u32[]{:S(2)}, u32[]{:S(2)}) %collective-permute-start.13) | collective-permute-done | bytes 524320 | tf_op jit(solution)/shard_map/ppermute | solution.py:16
  187.7 11.8 %psum.71 = f32[8]{0:T(128)S(1)} all-reduce(f32[8]{0:T(128)S(1)} %fusion.19), channel_id=1, replica_groups=mesh['pat'=4,'vox'=8] {'vox'}, use_global_device_ids=true, to_apply=%region_18.19 | all-reduce | flops 8 | bytes 64 | tf_op jit(solution)/shard_map/psum | solution.py:61
  202.9 2.4 collective-permute-start.15
  206.2 17.4 %collective-permute-done.14 = f32[1,16,128,128]{3,2,1,0:T(8,128)S(1)} collective-permute-done((f32[1,16,128,128]{3,2,1,0:T(8,128)S(1)}, f32[1,16,128,128]{3,2,1,0:T(8,128)S(1)}, u32[]{:S(2)}, u32[]{:S(2)}) %collective-permute-start.14) | collective-permute-done | bytes 1048608 | tf_op jit(solution)/shard_map/ppermute | solution.py:19
  223.6 4.9 %collective-permute-done.15 = f32[1,16,128,128]{3,2,1,0:T(8,128)S(1)} collective-permute-done((f32[1,16,128,128]{3,2,1,0:T(8,128)S(1)}, f32[1,16,128,128]{3,2,1,0:T(8,128)S(1)}, u32[]{:S(2)}, u32[]{:S(2)}) %collective-permute-start.15) | collective-permute-done | bytes 1048608 | tf_op jit(solution)/shard_map/ppermute | solution.py:16
  231.8 3.4 %collective-permute-done.16 = f32[2,128,128]{2,1,0:T(8,128)S(1)} collective-permute-done((f32[2,128,128]{2,1,0:T(8,128)S(1)}, f32[2,128,128]{2,1,0:T(8,128)S(1)}, u32[]{:S(2)}, u32[]{:S(2)}) %collective-permute-start.16) | collective-permute-done | bytes 131104 | tf_op jit(solution)/shard_map/ppermute | solution.py:154
  235.2 3.2 %collective-permute-start.17 = (f32[2,128,128]{2,1,0:T(8,128)S(1)}, f32[2,128,128]{2,1,0:T(8,128)S(1)}, u32[]{:S(2)}, u32[]{:S(2)}) collective-permute-start(f32[2,128,128]{2,1,0:T(8,128)S(1)} %add.274), channel_id=1, source_target_pairs={{0,16},{8,24},{16,0},{24,8},{1,17},{9,25},{17,1},{25,9},{2,18},{10... | collective-permute-start | bytes 393224 | tf_op jit(solution)/shard_map/ppermute | solution.py:154
  238.4 4.4 %collective-permute-done.17 = f32[2,128,128]{2,1,0:T(8,128)S(1)} collective-permute-done((f32[2,128,128]{2,1,0:T(8,128)S(1)}, f32[2,128,128]{2,1,0:T(8,128)S(1)}, u32[]{:S(2)}, u32[]{:S(2)}) %collective-permute-start.17) | collective-permute-done | bytes 131104 | tf_op jit(solution)/shard_map/ppermute | solution.py:154
  (114 shorter events, 44.7 us)
Async XLA Ops:
  0.6 14.4 %copy-start = (f32[2,8,128,128]{3,2,1,0:T(8,128)S(1)}, f32[2,8,128,128]{3,2,1,0:T(8,128)}, u32[]{:S(2)}) copy-start(f32[2,8,128,128]{3,2,1,0:T(8,128)} %param.8) | copy-start | bytes 3145732
  1.6 18.2 %collective-permute-start = (f32[1,128,128]{2,1,0:T(8,128)S(1)}, f32[1,128,128]{2,1,0:T(8,128)S(1)}, u32[]{:S(2)}, u32[]{:S(2)}) collective-permute-start(f32[1,128,128]{2,1,0:T(8,128)S(1)} %get-tuple-element.43), channel_id=1, source_target_pairs={{1,0},{2,1},{3,2},{4,3},{5,4},{6,5},{7,6},{9,8},{10,9},{11,10},{12... | collective-permute-start | bytes 196616 | tf_op jit(solution)/shard_map/ppermute | solution.py:19
  4.4 15.4 %collective-permute-start.1 = (f32[1,128,128]{2,1,0:T(8,128)S(1)}, f32[1,128,128]{2,1,0:T(8,128)S(1)}, u32[]{:S(2)}, u32[]{:S(2)}) collective-permute-start(f32[1,128,128]{2,1,0:T(8,128)S(1)} %get-tuple-element.42), channel_id=1, source_target_pairs={{0,1},{1,2},{2,3},{3,4},{4,5},{5,6},{6,7},{8,9},{9,10},{10,11},{11... | collective-permute-start | bytes 196616 | tf_op jit(solution)/shard_map/ppermute | solution.py:16
  8.4 9.6 %copy-start.15 = (f32[2,128,128]{2,1,0:T(8,128)S(1)}, f32[2,128,128]{2,1,0:T(8,128)}, u32[]{:S(2)}) copy-start(f32[2,128,128]{2,1,0:T(8,128)} %param.6) | copy-start | bytes 393220
  8.4 10.5 %copy-start.17 = (s32[8,4]{0,1:T(4,128)S(1)}, s32[8,4]{0,1:T(4,128)}, u32[]{:S(2)}) copy-start(s32[8,4]{0,1:T(4,128)} %param.10) | copy-start | bytes 388
  8.4 10.5 %copy-start.18 = (s32[128]{0:T(128)S(1)}, s32[128]{0:T(128)}, u32[]{:S(2)}) copy-start(s32[128]{0:T(128)} %param.9) | copy-start | bytes 1540
  8.4 10.8 %copy-start.1 = (f32[2,8,128,128]{3,2,1,0:T(8,128)S(1)}, f32[2,8,128,128]{3,2,1,0:T(8,128)}, u32[]{:S(2)}) copy-start(f32[2,8,128,128]{3,2,1,0:T(8,128)} %param.7) | copy-start | bytes 3145732
  8.4 16.4 %collective-permute-start.2 = (f32[1,8,128,128]{3,2,1,0:T(8,128)}, f32[1,8,128,128]{3,2,1,0:T(8,128)}, u32[]{:S(2)}, u32[]{:S(2)}) collective-permute-start(f32[1,8,128,128]{3,2,1,0:T(8,128)} %get-tuple-element.33), channel_id=1, source_target_pairs={{1,0},{2,1},{3,2},{4,3},{5,4},{6,5},{7,6},{9,8},{10,9},{11,10},{12... | collective-permute-start | bytes 1572872 | tf_op jit(solution)/shard_map/ppermute | solution.py:19
  13.1 12.7 %collective-permute-start.3 = (f32[1,8,128,128]{3,2,1,0:T(8,128)S(1)}, f32[1,8,128,128]{3,2,1,0:T(8,128)}, u32[]{:S(2)}, u32[]{:S(2)}) collective-permute-start(f32[1,8,128,128]{3,2,1,0:T(8,128)S(1)} %get-tuple-element.32), channel_id=1, source_target_pairs={{0,1},{1,2},{2,3},{3,4},{4,5},{5,6},{6,7},{8,9},{9,10},{10,11},{11... | collective-permute-start | bytes 1572872 | tf_op jit(solution)/shard_map/ppermute | solution.py:16
  16.1 71.8 %collective-permute-start.9 = (f32[1,8,128,128]{3,2,1,0:T(8,128)}, f32[1,8,128,128]{3,2,1,0:T(8,128)}, u32[]{:S(2)}, u32[]{:S(2)}) collective-permute-start(f32[1,8,128,128]{3,2,1,0:T(8,128)} %get-tuple-element.34), channel_id=1, source_target_pairs={{0,1},{1,2},{2,3},{3,4},{4,5},{5,6},{6,7},{8,9},{9,10},{10,11},{11... | collective-permute-start | bytes 1572872 | tf_op jit(solution)/shard_map/ppermute | solution.py:16
  20.0 7.2 %copy-start.16 = (s32[2,128,128]{2,1,0:T(8,128)S(1)}, s32[2,128,128]{2,1,0:T(8,128)}, u32[]{:S(2)}) copy-start(s32[2,128,128]{2,1,0:T(8,128)} %iota_add_fusion) | copy-start | bytes 393220
  28.0 30.7 %copy-start.3 = (f32[2,8,128,128]{3,2,1,0:T(8,128)}, f32[2,8,128,128]{3,2,1,0:T(8,128)S(1)}, u32[]{:S(2)}) copy-start(f32[2,8,128,128]{3,2,1,0:T(8,128)S(1)} %get-tuple-element.19) | copy-start | bytes 3145732
  28.0 6.0 %copy-start.11 = (f32[2,128,127]{2,1,0:T(8,128)S(1)}, f32[2,128,127]{2,1,0:T(8,128)}, u32[]{:S(2)}) copy-start(f32[2,128,127]{2,1,0:T(8,128)} %copy-done.10) | copy-start | bytes 390148
  28.1 14.1 %collective-permute-start.4 = (f32[1,8,128,128]{3,2,1,0:T(8,128)S(1)}, f32[1,8,128,128]{3,2,1,0:T(8,128)S(1)}, u32[]{:S(2)}, u32[]{:S(2)}) collective-permute-start(f32[1,8,128,128]{3,2,1,0:T(8,128)S(1)} %get-tuple-element.31), channel_id=1, source_target_pairs={{1,0},{2,1},{3,2},{4,3},{5,4},{6,5},{7,6},{9,8},{10,9},{11,10},{12... | collective-permute-start | bytes 1572872 | tf_op jit(solution)/shard_map/ppermute | solution.py:19
  32.0 11.5 %collective-permute-start.5 = (f32[1,8,128,128]{3,2,1,0:T(8,128)S(1)}, f32[1,8,128,128]{3,2,1,0:T(8,128)S(1)}, u32[]{:S(2)}, u32[]{:S(2)}) collective-permute-start(f32[1,8,128,128]{3,2,1,0:T(8,128)S(1)} %get-tuple-element.30), channel_id=1, source_target_pairs={{0,1},{1,2},{2,3},{3,4},{4,5},{5,6},{6,7},{8,9},{9,10},{10,11},{11... | collective-permute-start | bytes 1572872 | tf_op jit(solution)/shard_map/ppermute | solution.py:16
  60.3 27.6 %collective-permute-start.8 = (f32[1,8,128,128]{3,2,1,0:T(8,128)}, f32[1,8,128,128]{3,2,1,0:T(8,128)}, u32[]{:S(2)}, u32[]{:S(2)}) collective-permute-start(f32[1,8,128,128]{3,2,1,0:T(8,128)} %get-tuple-element.35), channel_id=1, source_target_pairs={{1,0},{2,1},{3,2},{4,3},{5,4},{6,5},{7,6},{9,8},{10,9},{11,10},{12... | collective-permute-start | bytes 1572872 | tf_op jit(solution)/shard_map/ppermute | solution.py:19
  80.5 4.6 %copy-start.12 = (f32[2,128,127]{2,1,0:T(8,128)S(1)}, f32[2,128,127]{2,1,0:T(8,128)}, u32[]{:S(2)}) copy-start(f32[2,128,127]{2,1,0:T(8,128)} %copy-done.10) | copy-start | bytes 390148
  80.6 12.3 %collective-permute-start.6 = (f32[1,8,128,128]{3,2,1,0:T(8,128)S(1)}, f32[1,8,128,128]{3,2,1,0:T(8,128)S(1)}, u32[]{:S(2)}, u32[]{:S(2)}) collective-permute-start(f32[1,8,128,128]{3,2,1,0:T(8,128)S(1)} %get-tuple-element.29), channel_id=1, source_target_pairs={{1,0},{2,1},{3,2},{4,3},{5,4},{6,5},{7,6},{9,8},{10,9},{11,10},{12... | collective-permute-start | bytes 1572872 | tf_op jit(solution)/shard_map/ppermute | solution.py:19
  82.5 4.2 %copy-start.7 = (f32[2,127,128]{2,1,0:T(8,128)S(1)}, f32[2,127,128]{2,1,0:T(8,128)}, u32[]{:S(2)}) copy-start(f32[2,127,128]{2,1,0:T(8,128)} %copy-done.5) | copy-start | bytes 390148
  82.5 12.5 %collective-permute-start.7 = (f32[1,8,128,128]{3,2,1,0:T(8,128)S(1)}, f32[1,8,128,128]{3,2,1,0:T(8,128)S(1)}, u32[]{:S(2)}, u32[]{:S(2)}) collective-permute-start(f32[1,8,128,128]{3,2,1,0:T(8,128)S(1)} %get-tuple-element.28), channel_id=1, source_target_pairs={{0,1},{1,2},{2,3},{3,4},{4,5},{5,6},{6,7},{8,9},{9,10},{10,11},{11... | collective-permute-start | bytes 1572872 | tf_op jit(solution)/shard_map/ppermute | solution.py:16
  111.0 14.6 %copy-start.19 = (f32[8]{0:T(128)S(1)}, f32[8]{0:T(128)}, u32[]{:S(2)}) copy-start(f32[8]{0:T(128)} %param.11) | copy-start | bytes 100
  129.4 4.6 %copy-start.13 = (f32[2,128,127]{2,1,0:T(8,128)S(1)}, f32[2,128,127]{2,1,0:T(8,128)}, u32[]{:S(2)}) copy-start(f32[2,128,127]{2,1,0:T(8,128)} %copy-done.10) | copy-start | bytes 390148
  129.5 11.3 %collective-permute-start.10 = (f32[1,8,128,128]{3,2,1,0:T(8,128)S(1)}, f32[1,8,128,128]{3,2,1,0:T(8,128)S(1)}, u32[]{:S(2)}, u32[]{:S(2)}) collective-permute-start(f32[1,8,128,128]{3,2,1,0:T(8,128)S(1)} %get-tuple-element.27), channel_id=1, source_target_pairs={{1,0},{2,1},{3,2},{4,3},{5,4},{6,5},{7,6},{9,8},{10,9},{11,10},{12... | collective-permute-start | bytes 1572872 | tf_op jit(solution)/shard_map/ppermute | solution.py:19
  131.4 13.7 %collective-permute-start.11 = (f32[1,8,128,128]{3,2,1,0:T(8,128)S(1)}, f32[1,8,128,128]{3,2,1,0:T(8,128)S(1)}, u32[]{:S(2)}, u32[]{:S(2)}) collective-permute-start(f32[1,8,128,128]{3,2,1,0:T(8,128)S(1)} %get-tuple-element.26), channel_id=1, source_target_pairs={{0,1},{1,2},{2,3},{3,4},{4,5},{5,6},{6,7},{8,9},{9,10},{10,11},{11... | collective-permute-start | bytes 1572872 | tf_op jit(solution)/shard_map/ppermute | solution.py:16
  146.1 24.0 %copy-start.4 = (f32[2,8,128,128]{3,2,1,0:T(8,128)}, f32[2,8,128,128]{3,2,1,0:T(8,128)S(1)}, u32[]{:S(2)}) copy-start(f32[2,8,128,128]{3,2,1,0:T(8,128)S(1)} %get-tuple-element.12) | copy-start | bytes 3145732
  171.6 4.6 %copy-start.14 = (f32[2,128,127]{2,1,0:T(8,128)S(1)}, f32[2,128,127]{2,1,0:T(8,128)}, u32[]{:S(2)}) copy-start(f32[2,128,127]{2,1,0:T(8,128)} %copy-done.10) | copy-start | bytes 390148
  171.7 11.6 %collective-permute-start.12 = (f32[1,8,128,128]{3,2,1,0:T(8,128)S(1)}, f32[1,8,128,128]{3,2,1,0:T(8,128)S(1)}, u32[]{:S(2)}, u32[]{:S(2)}) collective-permute-start(f32[1,8,128,128]{3,2,1,0:T(8,128)S(1)} %get-tuple-element.25), channel_id=1, source_target_pairs={{1,0},{2,1},{3,2},{4,3},{5,4},{6,5},{7,6},{9,8},{10,9},{11,10},{12... | collective-permute-start | bytes 1572872 | tf_op jit(solution)/shard_map/ppermute | solution.py:19
  173.8 13.0 %collective-permute-start.13 = (f32[1,8,128,128]{3,2,1,0:T(8,128)S(1)}, f32[1,8,128,128]{3,2,1,0:T(8,128)S(1)}, u32[]{:S(2)}, u32[]{:S(2)}) collective-permute-start(f32[1,8,128,128]{3,2,1,0:T(8,128)S(1)} %get-tuple-element.24), channel_id=1, source_target_pairs={{0,1},{1,2},{2,3},{3,4},{4,5},{5,6},{6,7},{8,9},{9,10},{10,11},{11... | collective-permute-start | bytes 1572872 | tf_op jit(solution)/shard_map/ppermute | solution.py:16
  200.9 22.6 %collective-permute-start.14 = (f32[1,16,128,128]{3,2,1,0:T(8,128)S(1)}, f32[1,16,128,128]{3,2,1,0:T(8,128)S(1)}, u32[]{:S(2)}, u32[]{:S(2)}) collective-permute-start(f32[1,16,128,128]{3,2,1,0:T(8,128)S(1)} %get-tuple-element.22), channel_id=1, source_target_pairs={{1,0},{2,1},{3,2},{4,3},{5,4},{6,5},{7,6},{9,8},{10,9},{11,10},{12... | collective-permute-start | bytes 3145736 | tf_op jit(solution)/shard_map/ppermute | solution.py:19
  202.9 25.6 %collective-permute-start.15 = (f32[1,16,128,128]{3,2,1,0:T(8,128)S(1)}, f32[1,16,128,128]{3,2,1,0:T(8,128)S(1)}, u32[]{:S(2)}, u32[]{:S(2)}) collective-permute-start(f32[1,16,128,128]{3,2,1,0:T(8,128)S(1)} %get-tuple-element.23), channel_id=1, source_target_pairs={{0,1},{1,2},{2,3},{3,4},{4,5},{5,6},{6,7},{8,9},{9,10},{10,11},{11... | collective-permute-start | bytes 3145736 | tf_op jit(solution)/shard_map/ppermute | solution.py:16
  230.1 5.0 %collective-permute-start.16 = (f32[2,128,128]{2,1,0:T(8,128)S(1)}, f32[2,128,128]{2,1,0:T(8,128)S(1)}, u32[]{:S(2)}, u32[]{:S(2)}) collective-permute-start(f32[2,128,128]{2,1,0:T(8,128)S(1)} %fusion.48), channel_id=1, source_target_pairs={{0,8},{8,0},{16,24},{24,16},{1,9},{9,1},{17,25},{25,17},{2,10},{10... | collective-permute-start | bytes 393224 | tf_op jit(solution)/shard_map/ppermute | solution.py:154
  235.2 7.5 %collective-permute-start.17 = (f32[2,128,128]{2,1,0:T(8,128)S(1)}, f32[2,128,128]{2,1,0:T(8,128)S(1)}, u32[]{:S(2)}, u32[]{:S(2)}) collective-permute-start(f32[2,128,128]{2,1,0:T(8,128)S(1)} %add.274), channel_id=1, source_target_pairs={{0,16},{8,24},{16,0},{24,8},{1,17},{9,25},{17,1},{25,9},{2,18},{10... | collective-permute-start | bytes 393224 | tf_op jit(solution)/shard_map/ppermute | solution.py:154
  (7 other events, 16.6 us)
